TPU v7x, 32 devices: a whole 2x2x4 slice. The times are simulated.
32 devices in a mesh: row: 8 (over y, x, core), col: 4 (over z).
Axes of the slice: x: 2, y: 2, z: 4, core: 2. Of those that a mesh axis runs over, the one named last changes fastest.
Arguments:
- panel_rows: float32 [128, 1024], P('row', 'col'), may hold values from 0.1 to 10
- trans_bias: float32 [12288, 128], P('row'), may hold values from 0.002 to 0.05
- trans_rate: float32 [1024, 512], P('col'), may hold values from 0.0005 to 0.01
- likelihood: float32 [12288, 1024], P('row', 'col'), may hold values from 0.1 to 720
Outputs:
- posterior: float32 [12288, 1024], P('row', 'col')
All inputs are finite; a program needn't handle non-finite values.
Results may differ from a plain program's by a relative error of at most 0.00005.
Values sent between devices are 32-bit elements; how exact they have to be, the bound alone decides.
A program may use at most 64 MiB of HBM per device.

v0:
```python
import jax
import jax.numpy as jnp
from jax import lax
from jax.sharding import PartitionSpec as P


def from_behind(block, axis, distance):
    devices = range(lax.axis_size(axis))
    route = [((i - distance) % len(devices), i) for i in devices]
    return lax.ppermute(block, axis, route)


def panel_product(weights, piece_rows):
    return jnp.dot(
        weights, piece_rows, precision=lax.Precision.HIGHEST, preferred_element_type=jnp.float32
    )


def rate_product(source, weights):
    return lax.dot_general(
        source,
        weights,
        (((1,), (1,)), ((), ())),
        precision=lax.Precision.HIGHEST,
        preferred_element_type=jnp.float32,
    )


def shards(panel_rows, trans_bias, trans_rate, likelihood):
    width = panel_rows.shape[1]
    own_block = panel_product(trans_bias, lax.all_gather(panel_rows, "row", axis=0, tiled=True))
    next_block = from_behind(own_block, "col", -1)
    predicted = rate_product(own_block, trans_rate[:, :width]) + rate_product(
        next_block, trans_rate[:, width:]
    )
    weighted = likelihood * predicted
    total_mass = lax.psum(jnp.sum(weighted), ("row", "col"))
    cell_count = float(
        weighted.shape[0] * lax.axis_size("row") * weighted.shape[1] * lax.axis_size("col")
    )
    return weighted * (cell_count / total_mass)


def solution(mesh):
    placed = (P("row", "col"), P("row", None), P("col", None), P("row", "col"))
    return jax.shard_map(
        shards, mesh=mesh, in_specs=placed, out_specs=P("row", "col"), check_vma=False
    )
```

profile of v0, /device:TPU:0, one launch (start us, length us, event | category | flops | bytes accessed | tf_op | source)
XLA Modules:
  0.0 94.1 jit_solution(14622655809166940988)
XLA Ops:
  0.0 0.0 copy-start
  0.0 0.0 copy-start.2
  0.0 11.0 %all_gather.3 = f32[128,256]{1,0:T(8,128)S(1)} all-gather(f32[16,256]{1,0:T(8,128)} %param.4), channel_id=1, replica_groups=mesh['row'=8,'col'=4] {'row'}, dimensions={0}, use_global_device_ids=true | all-gather | bytes 147456 | tf_op jit(solution)/shard_map/all_gather | solution.py:31
  11.0 0.0 copy-done
  11.0 1.4 %fusion.5 = f32[1536,256]{1,0:T(8,128)S(1)} fusion(f32[1536,128]{1,0:T(8,128)S(1)} %copy-done, f32[128,256]{1,0:T(8,128)S(1)} %all_gather.3), kind=kOutput, calls=%fused_computation.7 | convolution fusion | flops 603979776 | bytes 2490368 | tf_op jit(solution)/shard_map/dot_general | solution.py:14
  12.4 0.0 copy-start.1
  12.4 3.7 %collective-permute-start = (f32[1536,256]{1,0:T(8,128)S(1)}, f32[1536,256]{1,0:T(8,128)S(1)}, u32[]{:S(2)}, u32[]{:S(2)}) collective-permute-start(f32[1536,256]{1,0:T(8,128)S(1)} %fusion.5), channel_id=1, source_target_pairs={{1,0},{2,1},{3,2},{0,3},{5,4},{6,5},{7,6},{4,7},{9,8},{10,9},{11,1... | collective-permute-start | bytes 4718600 | tf_op jit(solution)/shard_map/ppermute | solution.py:10
  16.0 0.0 copy-done.2
  16.0 1.5 %fusion.2 = f32[1536,256]{1,0:T(8,128)S(1)} fusion(f32[1536,256]{1,0:T(8,128)S(1)} %fusion.5, f32[256,512]{1,0:T(8,128)S(1)} %copy-done.2), kind=kOutput, calls=%fused_computation.4 | convolution fusion | flops 1207959552 | bytes 3407872 | tf_op jit(solution)/shard_map/dot_general | solution.py:20
  17.5 32.7 %collective-permute-done = f32[1536,256]{1,0:T(8,128)S(1)} collective-permute-done((f32[1536,256]{1,0:T(8,128)S(1)}, f32[1536,256]{1,0:T(8,128)S(1)}, u32[]{:S(2)}, u32[]{:S(2)}) %collective-permute-start) | collective-permute-done | bytes 1572896 | tf_op jit(solution)/shard_map/ppermute | solution.py:10
  50.2 0.0 copy-done.1
  50.2 2.2 %fusion.4 = (f32[]{:T(128)}, f32[1536,256]{1,0:T(8,128)S(1)}) fusion(f32[1536,256]{1,0:T(8,128)S(1)} %copy-done.1, f32[1536,256]{1,0:T(8,128)S(1)} %fusion.2, f32[1536,256]{1,0:T(8,128)S(1)} %collective-permute-done, f32[256,512]{1,0:T(8,128)S(1)} %copy-done.2), kind=kOutput, calls=%fused_computation.6 | convolution fusion | flops 1209139200 | bytes 6553604 | tf_op jit(solution)/shard_map/dot_general | solution.py:20
  52.3 39.9 %psum.7 = f32[]{:T(128)} all-reduce(f32[]{:T(128)} %get-tuple-element.5), channel_id=1, replica_groups=mesh['row'=8,'col'=4] {'row','col'}, use_global_device_ids=true, to_apply=%region_1.0 | all-reduce | flops 1 | bytes 8 | tf_op jit(solution)/shard_map/psum | solution.py:37
  92.9 1.2 %broadcast_multiply_fusion = f32[1536,256]{1,0:T(8,128)} fusion(f32[1536,256]{1,0:T(8,128)S(1)} %get-tuple-element.6, f32[]{:T(128)S(6)} %div.3), kind=kLoop, calls=%fused_computation.2 | loop fusion | flops 393216 | bytes 3145732 | tf_op jit(solution)/shard_map/mul | solution.py:41
Async XLA Ops:
  0.0 11.0 %copy-start = (f32[1536,128]{1,0:T(8,128)S(1)}, f32[1536,128]{1,0:T(8,128)}, u32[]{:S(2)}) copy-start(f32[1536,128]{1,0:T(8,128)} %param.5) | copy-start | bytes 2359300
  0.0 16.0 %copy-start.2 = (f32[256,512]{1,0:T(8,128)S(1)}, f32[256,512]{1,0:T(8,128)}, u32[]{:S(2)}) copy-start(f32[256,512]{1,0:T(8,128)} %param.6) | copy-start | bytes 1572868
  12.4 37.8 %copy-start.1 = (f32[1536,256]{1,0:T(8,128)S(1)}, f32[1536,256]{1,0:T(8,128)}, u32[]{:S(2)}) copy-start(f32[1536,256]{1,0:T(8,128)} %param.7) | copy-start | bytes 4718596
  12.4 37.8 %collective-permute-start = (f32[1536,256]{1,0:T(8,128)S(1)}, f32[1536,256]{1,0:T(8,128)S(1)}, u32[]{:S(2)}, u32[]{:S(2)}) collective-permute-start(f32[1536,256]{1,0:T(8,128)S(1)} %fusion.5), channel_id=1, source_target_pairs={{1,0},{2,1},{3,2},{0,3},{5,4},{6,5},{7,6},{4,7},{9,8},{10,9},{11,1... | collective-permute-start | bytes 4718600 | tf_op jit(solution)/shard_map/ppermute | solution.py:10
where the time goes:
time: 94.6 us; the launch traced here: 94.1 us
  blocking collectives  50.8 us (54%)
  waiting for transfers between devices  32.7 us (35%)
  matrix products  5 us (5%)
  starting transfers between devices  3.65 us (4%)
  other arithmetic  1.25 us (1%)
    psum x1, blocking collectives, shards(): total_mass = lax.psum(jnp.sum(weighted), ('row', 'col'))  39.9 us
    ppermute x1, waiting for transfers between devices, from_behind(): return lax.ppermute(block, axis, route)  32.7 us
    all_gather x1, blocking collectives, shards(): lax.all_gather(panel_rows, 'row', axis=0, tiled=True)  11 us
    ppermute x1, starting transfers between devices, from_behind(): return lax.ppermute(block, axis, route)  3.65 us
    dot_general x2, matrix products, rate_product(): lax.dot_general(source, weights, (((1,), (1,)), ((), ())), precision=lax....  3.63 us
  transfers between devices with their start and end apart: 1, of which 1 were waited for; matrix products, arithmetic and copies ran while one was open for 2% of the time, Pallas kernels for 0%

commit v1 on v0

v1 whole, which is shorter than its diff:
```python
import functools

import jax
import jax.numpy as jnp
from jax import lax
from jax.experimental import pallas as pl
from jax.experimental.pallas import tpu as pltpu
from jax.sharding import PartitionSpec as P

MESH = pl.DeviceIdType.MESH
HIGHEST = lax.Precision.HIGHEST
F32 = jnp.float32


def dot(a, b, contract):
    return lax.dot_general(
        a, b, ((contract[:1], contract[1:]), ((), ())),
        precision=HIGHEST, preferred_element_type=F32,
    )


def window_kernel(
    n_row, n_col, cells,
    p_hbm, t_hbm, r_hbm, l_hbm,
    w_ref, s_ref,
    p_buf, p_next, t_buf, r_buf, l_buf, g_out, g_in, m_buf, mass_out, mass_in,
    load_sems, p_send, p_recv, g_send, g_recv, m_send, m_recv, mass_send, mass_recv,
):
    i = lax.axis_index("row")
    j = lax.axis_index("col")
    rows, width = p_buf.shape
    n = n_row * n_col
    loads = [
        pltpu.make_async_copy(src, dst, load_sems.at[k])
        for k, (src, dst) in enumerate(
            [(t_hbm, t_buf), (l_hbm, l_buf), (p_hbm, p_buf), (r_hbm, r_buf)]
        )
    ]
    for load in loads:
        load.start()

    barrier = pltpu.get_barrier_semaphore()
    for d in range(1, n_row):
        pl.semaphore_signal(
            barrier, inc=1, device_id=(lax.rem(i + d, n_row), j), device_id_type=MESH
        )
    for d in range(1, n_col):
        pl.semaphore_signal(
            barrier, inc=1, device_id=(i, lax.rem(j + d, n_col)), device_id_type=MESH
        )
    pl.semaphore_wait(barrier, n_row - 1 + n_col - 1)

    next_copy = pltpu.make_async_remote_copy(
        src_ref=p_hbm, dst_ref=p_next, send_sem=p_send, recv_sem=p_recv,
        device_id=(i, lax.rem(j + n_col - 1, n_col)), device_id_type=MESH,
    )
    next_copy.start()

    loads[0].wait()
    loads[1].wait()
    g = dot(t_buf[...], l_buf[...], (0, 0))
    for q in range(n_row):
        g_out[q] = g[q * rows:(q + 1) * rows]
    for d in range(1, n_row):
        peer = lax.rem(i + d, n_row)
        pltpu.make_async_remote_copy(
            src_ref=g_out.at[peer], dst_ref=g_in.at[d - 1],
            send_sem=g_send, recv_sem=g_recv,
            device_id=(peer, j), device_id_type=MESH,
        ).start()

    loads[2].wait()
    loads[3].wait()
    m = dot(p_buf[...], r_buf[:, :width], (1, 1))
    next_copy.wait()
    m = m + dot(p_next[...], r_buf[:, width:], (1, 1))
    m_buf[i] = m
    for d in range(1, n_row):
        pltpu.make_async_remote_copy(
            src_ref=m_buf.at[i], dst_ref=m_buf.at[i],
            send_sem=m_send, recv_sem=m_recv,
            device_id=(lax.rem(i + d, n_row), j), device_id_type=MESH,
        ).start()

    pltpu.make_async_copy(g_in, g_in, g_recv).wait()
    g_sum = g_out[i]
    for d in range(1, n_row):
        g_sum = g_sum + g_in[d - 1]
    mass = jnp.sum(g_sum * m, axis=0, keepdims=True)
    mass = sum(mass[:, k:k + 128] for k in range(0, width, 128))
    mass_out[...] = mass
    me = i * n_col + j

    def send_mass(d, carry):
        peer = lax.rem(me + d, n)
        pltpu.make_async_remote_copy(
            src_ref=mass_out, dst_ref=mass_in.at[d - 1],
            send_sem=mass_send, recv_sem=mass_recv,
            device_id=(peer // n_col, lax.rem(peer, n_col)), device_id_type=MESH,
        ).start()
        return carry

    lax.fori_loop(1, n, send_mass, 0)

    others = m_buf.at[pl.ds(0, n_row - 1)]
    pltpu.make_async_copy(others, others, m_recv).wait()
    m_all = jnp.concatenate([m_buf[q] for q in range(n_row)], axis=0)
    w_ref[...] = l_buf[...] * dot(t_buf[...], m_all, (1, 0))

    pltpu.make_async_copy(mass_in, mass_in, mass_recv).wait()
    total = jnp.sum(mass + jnp.sum(mass_in[...], axis=0))
    s_ref[...] = jnp.full(s_ref.shape, cells, F32) / total

    pltpu.make_async_copy(g_in, g_in, g_send).wait()
    pltpu.make_async_copy(others, others, m_send).wait()
    pltpu.make_async_copy(mass_in, mass_in, mass_send).wait()


def shards(panel_rows, trans_bias, trans_rate, likelihood):
    n_row, n_col = lax.axis_size("row"), lax.axis_size("col")
    rows, width = panel_rows.shape
    cells = float(likelihood.shape[0] * n_row * likelihood.shape[1] * n_col)
    dma = pltpu.SemaphoreType.DMA
    weighted, scale = pl.pallas_call(
        functools.partial(window_kernel, n_row, n_col, cells),
        out_shape=(
            jax.ShapeDtypeStruct(likelihood.shape, F32),
            jax.ShapeDtypeStruct((1, 128), F32),
        ),
        in_specs=[pl.BlockSpec(memory_space=pl.ANY)] * 4,
        out_specs=(
            pl.BlockSpec(memory_space=pltpu.VMEM),
            pl.BlockSpec(memory_space=pltpu.VMEM),
        ),
        scratch_shapes=[
            pltpu.VMEM((rows, width), F32),
            pltpu.VMEM((rows, width), F32),
            pltpu.VMEM(trans_bias.shape, F32),
            pltpu.VMEM(trans_rate.shape, F32),
            pltpu.VMEM(likelihood.shape, F32),
            pltpu.VMEM((n_row, rows, width), F32),
            pltpu.VMEM((n_row - 1, rows, width), F32),
            pltpu.VMEM((n_row, rows, width), F32),
            pltpu.VMEM((1, 128), F32),
            pltpu.VMEM((n_row * n_col - 1, 1, 128), F32),
            dma((4,)), dma, dma, dma, dma, dma, dma, dma, dma,
        ],
        compiler_params=pltpu.CompilerParams(collective_id=0, has_side_effects=True, vmem_limit_bytes=24 * 2**20),
        name="window",
    )(panel_rows, trans_bias, trans_rate, likelihood)
    return weighted * scale[0, 0]


def solution(mesh):
    placed = (P("row", "col"), P("row", None), P("col", None), P("row", "col"))
    return jax.shard_map(
        shards, mesh=mesh, in_specs=placed, out_specs=P("row", "col"), check_vma=False
    )
```

time: 94.6 us -> 21.6 us (0.23)
  blocking collectives: 50.8 us -> 0 us
  waiting for transfers between devices: 32.7 us -> 0 us
  Pallas kernels: 0 us -> 15.7 us
  matrix products: 5 us -> 0 us
  local copies, waits for them, and re-layouts: 0.01 us -> 4.3 us
  starting transfers between devices: 3.65 us -> 0 us
    psum x1 -> x0, blocking collectives: 39.9 us -> none  [shards(): total_mass = lax.psum(jnp.sum(weighted), ('row', 'col'))]
    ppermute x1 -> x0, waiting for transfers between devices: 32.7 us -> none  [from_behind(): return lax.ppermute(block, axis, route)]
    pallas_call x0 -> x1, Pallas kernels: none -> 15.7 us  [shards(): pl.pallas_call(functools.partial(window_kernel, n_row, n_col, cells), out...]
    all_gather x1 -> x0, blocking collectives: 11 us -> none  [shards(): lax.all_gather(panel_rows, 'row', axis=0, tiled=True)]
    dot_general x3 -> x0, matrix products: 5 us -> none  [the longest x2 3.63 us: rate_product(): lax.dot_general(source, weights, (((1,), (1,)), ((), ())), precision=lax....]
    unnamed x6 -> x8, local copies, waits for them, and re-layouts: 0.01 us -> 4.3 us
    ppermute x1 -> x0, starting transfers between devices: 3.65 us -> none  [from_behind(): return lax.ppermute(block, axis, route)]
  transfers between devices with their start and end apart: 1 -> 0, of which waited for: 1 -> 0; matrix products, arithmetic and copies ran while one was open for 2% -> 0% of each run, Pallas kernels for 0% -> 0%
where the time goes in v1:
time: 21.6 us; the launch traced here: 21.3 us
  Pallas kernels  15.7 us (73%)
  local copies, waits for them, and re-layouts  4.3 us (20%)
  other arithmetic  1.28 us (6%)
    pallas_call x1, Pallas kernels, shards(): pl.pallas_call(functools.partial(window_kernel, n_row, n_col, cells), out...  15.7 us
    unnamed x8, local copies, waits for them, and re-layouts  4.3 us
    mul x1, other arithmetic, shards(): return weighted * scale[0, 0]  1.28 us

profile of v1, /device:TPU:0, one launch (start us, length us, event | category | flops | bytes accessed | tf_op | source)
XLA Modules:
  0.0 21.3 jit_solution(1699690218646076315)
XLA Ops:
  0.0 0.0 copy-start
  0.0 1.4 %copy-done = f32[1536,256]{1,0:T(8,128)S(1)} copy-done((f32[1536,256]{1,0:T(8,128)S(1)}, f32[1536,256]{1,0:T(8,128)}, u32[]{:S(2)}) %copy-start) | copy-done | bytes 1572888
  1.4 0.0 copy-start.1
  1.4 1.1 %copy-done.1 = f32[1536,128]{1,0:T(8,128)S(1)} copy-done((f32[1536,128]{1,0:T(8,128)S(1)}, f32[1536,128]{1,0:T(8,128)}, u32[]{:S(2)}) %copy-start.1) | copy-done | bytes 786456
  2.5 0.0 copy-start.2
  2.5 1.0 %copy-done.2 = f32[256,512]{1,0:T(8,128)S(1)} copy-done((f32[256,512]{1,0:T(8,128)S(1)}, f32[256,512]{1,0:T(8,128)}, u32[]{:S(2)}) %copy-start.2) | copy-done | bytes 524312
  3.6 0.0 copy-start.3
  3.6 0.7 %copy-done.3 = f32[16,256]{1,0:T(8,128)S(1)} copy-done((f32[16,256]{1,0:T(8,128)S(1)}, f32[16,256]{1,0:T(8,128)}, u32[]{:S(2)}) %copy-start.3) | copy-done | bytes 16408
  4.3 15.7 %window.1 = (f32[1536,256]{1,0:T(8,128)S(1)}, f32[1,128]{1,0:T(1,128)S(1)}) custom-call(f32[16,256]{1,0:T(8,128)S(1)} %copy-done.3, f32[1536,128]{1,0:T(8,128)S(1)} %copy-done.1, f32[256,512]{1,0:T(8,128)S(1)} %copy-done.2, f32[1536,256]{1,0:T(8,128)S(1)} %copy-done), custom_call_target="tpu_custom_call" | custom-call | tf_op jit(solution)/shard_map/window/pallas_call | solution.py:124
  20.0 1.3 %broadcast_multiply_fusion = f32[1536,256]{1,0:T(8,128)} fusion(f32[1536,256]{1,0:T(8,128)S(1)} %get-tuple-element.7, f32[]{:T(128)S(1)} %bitcast.2), kind=kLoop, calls=%fused_computation | loop fusion | flops 393216 | bytes 3145732 | tf_op jit(solution)/shard_map/mul | solution.py:151
Async XLA Ops:
  0.0 1.4 %copy-start = (f32[1536,256]{1,0:T(8,128)S(1)}, f32[1536,256]{1,0:T(8,128)}, u32[]{:S(2)}) copy-start(f32[1536,256]{1,0:T(8,128)} %l_hbm.1) | copy-start | bytes 4718596
  1.4 1.1 %copy-start.1 = (f32[1536,128]{1,0:T(8,128)S(1)}, f32[1536,128]{1,0:T(8,128)}, u32[]{:S(2)}) copy-start(f32[1536,128]{1,0:T(8,128)} %t_hbm.1) | copy-start | bytes 2359300
  2.5 1.0 %copy-start.2 = (f32[256,512]{1,0:T(8,128)S(1)}, f32[256,512]{1,0:T(8,128)}, u32[]{:S(2)}) copy-start(f32[256,512]{1,0:T(8,128)} %r_hbm.1) | copy-start | bytes 1572868
  3.6 0.7 %copy-start.3 = (f32[16,256]{1,0:T(8,128)S(1)}, f32[16,256]{1,0:T(8,128)}, u32[]{:S(2)}) copy-start(f32[16,256]{1,0:T(8,128)} %p_hbm.1) | copy-start | bytes 49156

commit v2 on v1

v2 whole, which is shorter than its diff:
```python
import functools

import jax
import jax.numpy as jnp
from jax import lax
from jax.experimental import pallas as pl
from jax.experimental.pallas import tpu as pltpu
from jax.sharding import PartitionSpec as P

MESH = pl.DeviceIdType.MESH
F32 = jnp.float32


def split(x):
    high = x.astype(jnp.bfloat16)
    return high, (x - high.astype(F32)).astype(jnp.bfloat16)


def dot_bf16(a, b, contract):
    return lax.dot_general(
        a, b, ((contract[:1], contract[1:]), ((), ())), preferred_element_type=F32
    )


def wrapped(position, size):
    return jnp.where(position >= size, position - size, position)


def window_kernel(
    n_row, n_col, cells,
    p_hbm, t_hbm, r_hbm, l_hbm,
    w_ref, s_ref,
    p_buf, p_next, t_buf, t_parts, r_buf, r_parts, l_buf, g_out, g_in, m_buf, mass_out, mass_in,
    load_sems, p_send, p_recv, g_send, g_recv, m_send, m_recv, mass_send, mass_recv,
):
    i = lax.axis_index("row")
    j = lax.axis_index("col")
    rows, width = p_buf.shape
    row_of = [i] + [wrapped(i + d, n_row) for d in range(1, n_row)]
    col_of = [j] + [wrapped(j + d, n_col) for d in range(1, n_col)]
    loads = [
        pltpu.make_async_copy(src, dst, load_sems.at[k])
        for k, (src, dst) in enumerate(
            [(t_hbm, t_buf), (l_hbm, l_buf), (p_hbm, p_buf), (r_hbm, r_buf)]
        )
    ]
    for load in loads:
        load.start()

    barrier = pltpu.get_barrier_semaphore()
    for d in range(1, n_row):
        pl.semaphore_signal(
            barrier, inc=1, device_id=(row_of[d], j), device_id_type=MESH
        )
    for d in range(1, n_col):
        pl.semaphore_signal(
            barrier, inc=1, device_id=(i, col_of[d]), device_id_type=MESH
        )
    loads[0].wait()
    loads[1].wait()
    depth = t_buf.shape[1]
    t_high, t_low = split(t_buf[...])
    t_parts[:, :depth] = t_high
    t_parts[:, depth:] = t_low
    l_high, l_low = split(l_buf[...])
    g = dot_bf16(t_parts[...], l_high, (0, 0))
    g = g[:depth] + g[depth:] + dot_bf16(t_parts[:, :depth], l_low, (0, 0))
    for q in range(n_row):
        g_out[q] = g[q * rows:(q + 1) * rows]
    pl.semaphore_wait(barrier, n_row - 1 + n_col - 1)

    next_copy = pltpu.make_async_remote_copy(
        src_ref=p_hbm, dst_ref=p_next, send_sem=p_send, recv_sem=p_recv,
        device_id=(i, col_of[n_col - 1]), device_id_type=MESH,
    )
    next_copy.start()

    for d in range(1, n_row):
        peer = row_of[d]
        pltpu.make_async_remote_copy(
            src_ref=g_out.at[peer], dst_ref=g_in.at[d - 1],
            send_sem=g_send, recv_sem=g_recv,
            device_id=(peer, j), device_id_type=MESH,
        ).start()

    loads[2].wait()
    loads[3].wait()
    r_high, r_low = split(r_buf[...].T)
    r_parts[0] = r_high
    r_parts[1] = r_low

    def rate_rows(p_rows, start):
        p_high, p_low = split(p_rows)
        high = r_parts[0, start:start + width]
        low = r_parts[1, start:start + width]
        return (
            dot_bf16(p_high, low, (1, 0)) + dot_bf16(p_low, high, (1, 0))
            + dot_bf16(p_high, high, (1, 0))
        )

    m = rate_rows(p_buf[...], 0)
    next_copy.wait()
    m = m + rate_rows(p_next[...], width)
    m_buf[i] = m
    for d in range(1, n_row):
        pltpu.make_async_remote_copy(
            src_ref=m_buf.at[i], dst_ref=m_buf.at[i],
            send_sem=m_send, recv_sem=m_recv,
            device_id=(row_of[d], j), device_id_type=MESH,
        ).start()

    pltpu.make_async_copy(g_in, g_in, g_recv).wait()
    g_sum = g_out[i]
    for d in range(1, n_row):
        g_sum = g_sum + g_in[d - 1]
    mass = jnp.sum(g_sum * m, axis=0, keepdims=True)
    mass = sum(mass[:, k:k + 128] for k in range(0, width, 128))
    mass_out[...] = mass

    def send_mass(row, first, from_col):
        for d in range(from_col, n_col):
            pltpu.make_async_remote_copy(
                src_ref=mass_out, dst_ref=mass_in.at[first + d - 1],
                send_sem=mass_send, recv_sem=mass_recv,
                device_id=(row, col_of[d]), device_id_type=MESH,
            ).start()

    if n_row * n_col <= 64:
        for d in reversed(range(1, n_row)):
            send_mass(row_of[d], d * n_col, 0)
    else:

        def send_row(d, carry):
            send_mass(wrapped(i + d, n_row), d * n_col, 0)
            return carry

        lax.fori_loop(1, n_row, send_row, 0)
    send_mass(i, 0, 1)

    others = m_buf.at[pl.ds(0, n_row - 1)]
    pltpu.make_async_copy(others, others, m_recv).wait()
    m_all = jnp.concatenate([m_buf[q] for q in range(n_row)], axis=0)
    m_high, m_low = split(m_all)
    predicted = dot_bf16(t_parts[...], jnp.concatenate([m_high, m_high], axis=0), (1, 0))
    predicted = predicted + dot_bf16(t_parts[:, :depth], m_low, (1, 0))
    w_ref[...] = l_buf[...] * predicted

    pltpu.make_async_copy(mass_in, mass_in, mass_recv).wait()
    total = jnp.sum(mass + jnp.sum(mass_in[...], axis=0))
    s_ref[...] = jnp.full(s_ref.shape, cells, F32) / total

    pltpu.make_async_copy(g_in, g_in, g_send).wait()
    pltpu.make_async_copy(others, others, m_send).wait()
    pltpu.make_async_copy(mass_in, mass_in, mass_send).wait()


def shards(panel_rows, trans_bias, trans_rate, likelihood):
    n_row, n_col = lax.axis_size("row"), lax.axis_size("col")
    rows, width = panel_rows.shape
    cells = float(likelihood.shape[0] * n_row * likelihood.shape[1] * n_col)
    dma = pltpu.SemaphoreType.DMA
    weighted, scale = pl.pallas_call(
        functools.partial(window_kernel, n_row, n_col, cells),
        out_shape=(
            jax.ShapeDtypeStruct(likelihood.shape, F32),
            jax.ShapeDtypeStruct((1, 128), F32),
        ),
        in_specs=[pl.BlockSpec(memory_space=pltpu.HBM)] * 4,
        out_specs=(
            pl.BlockSpec(memory_space=pltpu.VMEM),
            pl.BlockSpec(memory_space=pltpu.VMEM),
        ),
        scratch_shapes=[
            pltpu.VMEM((rows, width), F32),
            pltpu.VMEM((rows, width), F32),
            pltpu.VMEM(trans_bias.shape, F32),
            pltpu.VMEM((trans_bias.shape[0], 2 * trans_bias.shape[1]), jnp.bfloat16),
            pltpu.VMEM(trans_rate.shape, F32),
            pltpu.VMEM((2,) + trans_rate.shape[::-1], jnp.bfloat16),
            pltpu.VMEM(likelihood.shape, F32),
            pltpu.VMEM((n_row, rows, width), F32),
            pltpu.VMEM((n_row - 1, rows, width), F32),
            pltpu.VMEM((n_row, rows, width), F32),
            pltpu.VMEM((1, 128), F32),
            pltpu.VMEM((n_row * n_col - 1, 1, 128), F32),
            dma((4,)), dma, dma, dma, dma, dma, dma, dma, dma,
        ],
        compiler_params=pltpu.CompilerParams(collective_id=0, has_side_effects=True, vmem_limit_bytes=24 * 2**20),
        name="window",
    )(*[pltpu.with_memory_space_constraint(x, pltpu.HBM) for x in (panel_rows, trans_bias, trans_rate, likelihood)])
    return weighted * scale[0, 0]


def solution(mesh):
    placed = (P("row", "col"), P("row", None), P("col", None), P("row", "col"))
    return jax.shard_map(
        shards, mesh=mesh, in_specs=placed, out_specs=P("row", "col"), check_vma=False
    )
```

time: 21.6 us -> 16.3 us (0.75)
  local copies, waits for them, and re-layouts: 4.3 us -> 0 us
  Pallas kernels: 15.7 us -> 14.9 us
    unnamed x8 -> x0, local copies, waits for them, and re-layouts: 4.3 us -> none
    pallas_call x1, Pallas kernels: 15.7 us -> 14.9 us  [shards(): pl.pallas_call(functools.partial(window_kernel, n_row, n_col, cells), out...]
where the time goes in v2:
time: 16.3 us; the launch traced here: 16.1 us
  Pallas kernels  14.9 us (91%)
  other arithmetic  1.28 us (8%)
    pallas_call x1, Pallas kernels, shards(): pl.pallas_call(functools.partial(window_kernel, n_row, n_col, cells), out...  14.9 us
    mul x1, other arithmetic, shards(): return weighted * scale[0, 0]  1.28 us

profile of v2, /device:TPU:0, one launch (start us, length us, event | category | flops | bytes accessed | tf_op | source)
XLA Modules:
  0.0 16.1 jit_solution(9637810168102213609)
XLA Ops:
  0.0 14.9 %window.1 = (f32[1536,256]{1,0:T(8,128)S(1)}, f32[1,128]{1,0:T(1,128)S(1)}) custom-call(f32[16,256]{1,0:T(8,128)} %p_hbm.1, f32[1536,128]{1,0:T(8,128)} %t_hbm.1, f32[256,512]{1,0:T(8,128)} %r_hbm.1, f32[1536,256]{1,0:T(8,128)} %l_hbm.1), custom_call_target="tpu_custom_call" | custom-call | tf_op jit(solution)/shard_map/window/pallas_call | solution.py:162
  14.9 1.3 %broadcast_multiply_fusion = f32[1536,256]{1,0:T(8,128)} fusion(f32[1536,256]{1,0:T(8,128)S(1)} %get-tuple-element.7, f32[]{:T(128)S(1)} %bitcast.2), kind=kLoop, calls=%fused_computation | loop fusion | flops 393216 | bytes 3145732 | tf_op jit(solution)/shard_map/mul | solution.py:191

commit v3 on v2

--- a/solution.py
+++ b/solution.py
@@ -9,6 +9,7 @@
 
 MESH = pl.DeviceIdType.MESH
 F32 = jnp.float32
+PIECES = 1
 
 
 def split(x):
@@ -38,14 +39,24 @@
     rows, width = p_buf.shape
     row_of = [i] + [wrapped(i + d, n_row) for d in range(1, n_row)]
     col_of = [j] + [wrapped(j + d, n_col) for d in range(1, n_col)]
-    loads = [
-        pltpu.make_async_copy(src, dst, load_sems.at[k])
-        for k, (src, dst) in enumerate(
-            [(t_hbm, t_buf), (l_hbm, l_buf), (p_hbm, p_buf), (r_hbm, r_buf)]
-        )
+    depth = t_buf.shape[1]
+    height = t_buf.shape[0] // PIECES
+    pieces = [pl.ds(k * height, height) for k in range(PIECES)]
+    p_load = pltpu.make_async_copy(p_hbm, p_buf, load_sems.at[0])
+    r_load = pltpu.make_async_copy(r_hbm, r_buf, load_sems.at[1])
+    t_loads = [
+        pltpu.make_async_copy(t_hbm.at[piece], t_buf.at[piece], load_sems.at[2 + k])
+        for k, piece in enumerate(pieces)
     ]
-    for load in loads:
-        load.start()
+    l_loads = [
+        pltpu.make_async_copy(l_hbm.at[piece], l_buf.at[piece], load_sems.at[2 + PIECES + k])
+        for k, piece in enumerate(pieces)
+    ]
+    p_load.start()
+    for t_load, l_load in zip(t_loads, l_loads):
+        t_load.start()
+        l_load.start()
+    r_load.start()
 
     barrier = pltpu.get_barrier_semaphore()
     for d in range(1, n_row):
@@ -56,35 +67,21 @@
         pl.semaphore_signal(
             barrier, inc=1, device_id=(i, col_of[d]), device_id_type=MESH
         )
-    loads[0].wait()
-    loads[1].wait()
-    depth = t_buf.shape[1]
-    t_high, t_low = split(t_buf[...])
-    t_parts[:, :depth] = t_high
-    t_parts[:, depth:] = t_low
-    l_high, l_low = split(l_buf[...])
-    g = dot_bf16(t_parts[...], l_high, (0, 0))
-    g = g[:depth] + g[depth:] + dot_bf16(t_parts[:, :depth], l_low, (0, 0))
+    g = None
+    for piece, t_load, l_load in zip(pieces, t_loads, l_loads):
+        t_load.wait()
+        t_high, t_low = split(t_buf[piece])
+        t_parts[piece, :depth] = t_high
+        t_parts[piece, depth:] = t_low
+        l_load.wait()
+        l_high, l_low = split(l_buf[piece])
+        both = dot_bf16(t_parts[piece], l_high, (0, 0))
+        part = both[:depth] + both[depth:] + dot_bf16(t_high, l_low, (0, 0))
+        g = part if g is None else g + part
     for q in range(n_row):
         g_out[q] = g[q * rows:(q + 1) * rows]
-    pl.semaphore_wait(barrier, n_row - 1 + n_col - 1)
-
-    next_copy = pltpu.make_async_remote_copy(
-        src_ref=p_hbm, dst_ref=p_next, send_sem=p_send, recv_sem=p_recv,
-        device_id=(i, col_of[n_col - 1]), device_id_type=MESH,
-    )
-    next_copy.start()
-
-    for d in range(1, n_row):
-        peer = row_of[d]
-        pltpu.make_async_remote_copy(
-            src_ref=g_out.at[peer], dst_ref=g_in.at[d - 1],
-            send_sem=g_send, recv_sem=g_recv,
-            device_id=(peer, j), device_id_type=MESH,
-        ).start()
-
-    loads[2].wait()
-    loads[3].wait()
+    p_load.wait()
+    r_load.wait()
     r_high, r_low = split(r_buf[...].T)
     r_parts[0] = r_high
     r_parts[1] = r_low
@@ -99,6 +96,22 @@
         )
 
     m = rate_rows(p_buf[...], 0)
+    pl.semaphore_wait(barrier, n_row - 1 + n_col - 1)
+
+    next_copy = pltpu.make_async_remote_copy(
+        src_ref=p_buf, dst_ref=p_next, send_sem=p_send, recv_sem=p_recv,
+        device_id=(i, col_of[n_col - 1]), device_id_type=MESH,
+    )
+    next_copy.start()
+
+    for d in range(1, n_row):
+        peer = row_of[d]
+        pltpu.make_async_remote_copy(
+            src_ref=g_out.at[peer], dst_ref=g_in.at[d - 1],
+            send_sem=g_send, recv_sem=g_recv,
+            device_id=(peer, j), device_id_type=MESH,
+        ).start()
+
     next_copy.wait()
     m = m + rate_rows(p_next[...], width)
     m_buf[i] = m
@@ -183,7 +196,7 @@
             pltpu.VMEM((n_row, rows, width), F32),
             pltpu.VMEM((1, 128), F32),
             pltpu.VMEM((n_row * n_col - 1, 1, 128), F32),
-            dma((4,)), dma, dma, dma, dma, dma, dma, dma, dma,
+            dma((2 + 2 * PIECES,)), dma, dma, dma, dma, dma, dma, dma, dma,
         ],
         compiler_params=pltpu.CompilerParams(collective_id=0, has_side_effects=True, vmem_limit_bytes=24 * 2**20),
         name="window",

time: 16.3 us -> 16.1 us (0.988)
  Pallas kernels: 14.9 us -> 14.6 us
    pallas_call x1, Pallas kernels: 14.9 us -> 14.6 us  [shards(): pl.pallas_call(functools.partial(window_kernel, n_row, n_col, cells), out...]
where the time goes in v3:
time: 16.1 us; the launch traced here: 15.9 us
  Pallas kernels  14.6 us (91%)
  other arithmetic  1.28 us (8%)
    pallas_call x1, Pallas kernels, shards(): pl.pallas_call(functools.partial(window_kernel, n_row, n_col, cells), out...  14.6 us
    mul x1, other arithmetic, shards(): return weighted * scale[0, 0]  1.28 us

profile of v3, /device:TPU:0, one launch (start us, length us, event | category | flops | bytes accessed | tf_op | source)
XLA Modules:
  0.0 15.9 jit_solution(3286678425174146218)
XLA Ops:
  0.0 14.6 %window.1 = (f32[1536,256]{1,0:T(8,128)S(1)}, f32[1,128]{1,0:T(1,128)S(1)}) custom-call(f32[16,256]{1,0:T(8,128)} %p_hbm.1, f32[1536,128]{1,0:T(8,128)} %t_hbm.1, f32[256,512]{1,0:T(8,128)} %r_hbm.1, f32[1536,256]{1,0:T(8,128)} %l_hbm.1), custom_call_target="tpu_custom_call" | custom-call | tf_op jit(solution)/shard_map/window/pallas_call | solution.py:175
  14.7 1.3 %broadcast_multiply_fusion = f32[1536,256]{1,0:T(8,128)} fusion(f32[1536,256]{1,0:T(8,128)S(1)} %get-tuple-element.7, f32[]{:T(128)S(1)} %bitcast.2), kind=kLoop, calls=%fused_computation | loop fusion | flops 393216 | bytes 3145732 | tf_op jit(solution)/shard_map/mul | solution.py:204

commit v4 on v3

--- a/solution.py
+++ b/solution.py
@@ -37,6 +37,7 @@
     i = lax.axis_index("row")
     j = lax.axis_index("col")
     rows, width = p_buf.shape
+    far_first = sorted(range(1, n_row), key=lambda d: abs(2 * d - n_row))
     row_of = [i] + [wrapped(i + d, n_row) for d in range(1, n_row)]
     col_of = [j] + [wrapped(j + d, n_col) for d in range(1, n_col)]
     depth = t_buf.shape[1]
@@ -104,7 +105,7 @@
     )
     next_copy.start()
 
-    for d in range(1, n_row):
+    for d in far_first:
         peer = row_of[d]
         pltpu.make_async_remote_copy(
             src_ref=g_out.at[peer], dst_ref=g_in.at[d - 1],
@@ -115,7 +116,7 @@
     next_copy.wait()
     m = m + rate_rows(p_next[...], width)
     m_buf[i] = m
-    for d in range(1, n_row):
+    for d in far_first:
         pltpu.make_async_remote_copy(
             src_ref=m_buf.at[i], dst_ref=m_buf.at[i],
             send_sem=m_send, recv_sem=m_recv,

time: 16.1 us -> 16.1 us (level)
  no operation moved by 1% of the time
where the time goes in v4:
time: 16.1 us; the launch traced here: 15.9 us
  Pallas kernels  14.6 us (91%)
  other arithmetic  1.28 us (8%)
    pallas_call x1, Pallas kernels, shards(): pl.pallas_call(functools.partial(window_kernel, n_row, n_col, cells), out...  14.6 us
    mul x1, other arithmetic, shards(): return weighted * scale[0, 0]  1.28 us

profile of v4, /device:TPU:0, one launch (start us, length us, event | category | flops | bytes accessed | tf_op | source)
XLA Modules:
  0.0 15.9 jit_solution(15976189391140267499)
XLA Ops:
  0.0 14.6 %window.1 = (f32[1536,256]{1,0:T(8,128)S(1)}, f32[1,128]{1,0:T(1,128)S(1)}) custom-call(f32[16,256]{1,0:T(8,128)} %p_hbm.1, f32[1536,128]{1,0:T(8,128)} %t_hbm.1, f32[256,512]{1,0:T(8,128)} %r_hbm.1, f32[1536,256]{1,0:T(8,128)} %l_hbm.1), custom_call_target="tpu_custom_call" | custom-call | tf_op jit(solution)/shard_map/window/pallas_call | solution.py:176
  14.7 1.3 %broadcast_multiply_fusion = f32[1536,256]{1,0:T(8,128)} fusion(f32[1536,256]{1,0:T(8,128)S(1)} %get-tuple-element.7, f32[]{:T(128)S(1)} %bitcast.2), kind=kLoop, calls=%fused_computation | loop fusion | flops 393216 | bytes 3145732 | tf_op jit(solution)/shard_map/mul | solution.py:205
